TPU v7x, 256 devices: a whole 4x4x8 slice. The times are simulated.
256 devices in a mesh: seq: 8 (over z_hi, x), head: 32 (over y, z_lo, core).
Axes of the slice: x: 4, y: 4, z: 8 (z_hi: 2, z_lo: 4; z = z_hi * 4 + z_lo), core: 2. Of those that a mesh axis runs over, the one named last changes fastest.
Arguments:
- queries: bfloat16 [8192, 8192], P(('seq', 'head')), may hold values from -6 to 6
- keys: bfloat16 [8192, 8192], P(('seq', 'head')), may hold values from -6 to 6
- values: bfloat16 [8192, 8192], P(('seq', 'head')), may hold values from -6 to 6
- out_grad: bfloat16 [8192, 8192], P(('seq', 'head')), may hold values from -6 to 6
- selected: int32 [64, 16, 3], P('head', 'seq'), may hold values from 0 to 14, as said below
- length: int32 [1], replicated, may hold values from 4096 to 8192
Outputs:
- attended: bfloat16 [8192, 8192], P(('seq', 'head'))
- query_grad: bfloat16 [8192, 8192], P(('seq', 'head'))
- key_grad: bfloat16 [8192, 8192], P(('seq', 'head'))
- value_grad: bfloat16 [8192, 8192], P(('seq', 'head'))
Inputs may be any that keep to these rules, and one draw needn't show every extreme that they name: `selected`: for head h and query block b every entry lies in 0 to b; the entries below b are distinct, there are min(3, b) of them, and b-1 is one of them when b > 0; the other entries equal b.
All inputs are finite; a program needn't handle non-finite values.
Results may differ from a plain program's by a relative error of at most 0.012.
The roundings to bfloat16 on the way count: a program that leaves them out, or rounds other values in their place, can miss the bound.
Values may be sent and summed in bfloat16 or wider, within the bound.
A program may use at most 128 MiB of HBM per device.

v0:
```python
import math

import jax
import jax.numpy as jnp
from jax import lax
from jax.sharding import PartitionSpec as P

HD = 128
BLOCK = 512
TOP = 3


masked_score = -1e30


def usable_mask(chosen, block_id, row_count):
    whole = chosen < block_id
    remote = jnp.broadcast_to(whole[:, None], (chosen.shape[0], row_count)).reshape(1, -1)
    remote = jnp.broadcast_to(remote, (row_count, chosen.shape[0] * row_count))
    lower = jnp.arange(row_count)[None, :] <= jnp.arange(row_count)[:, None]
    return jnp.concatenate([remote, lower], axis=1)


def attend(query_rows, key_set, value_set, grad_rows, usable, live_rows):
    scaling = 1.0 / math.sqrt(query_rows.shape[-1])
    scores = jnp.dot(query_rows, key_set.T, preferred_element_type=jnp.float32) * scaling
    scores = jnp.where(usable, scores, masked_score)
    row_max = jnp.max(scores, axis=1, keepdims=True)
    raised = jnp.exp(scores - row_max)
    weights = raised / jnp.sum(raised, axis=1, keepdims=True)
    weights_low = weights.astype(jnp.bfloat16)
    output = jnp.dot(weights_low, value_set, preferred_element_type=jnp.float32)
    output = jnp.where(live_rows[:, None], output, 0.0).astype(jnp.bfloat16)
    grad_in = jnp.where(live_rows[:, None], grad_rows, jnp.zeros_like(grad_rows))
    dweights = jnp.dot(grad_in, value_set.T, preferred_element_type=jnp.float32)
    delta = jnp.sum(grad_in.astype(jnp.float32) * output.astype(jnp.float32), axis=1, keepdims=True)
    dscores = (weights * (dweights - delta) * scaling).astype(jnp.bfloat16)
    query_grad = jnp.dot(dscores, key_set, preferred_element_type=jnp.float32).astype(jnp.bfloat16)
    key_term = jnp.dot(dscores.T, query_rows, preferred_element_type=jnp.float32)
    value_term = jnp.dot(weights_low.T, grad_in, preferred_element_type=jnp.float32)
    return (output, query_grad, key_term, value_term)


def body(queries, keys, values, out_grad, selected, length):
    query_here, key_here, value_here, grad_here = (
        lax.all_to_all(queries, "head", split_axis=1, concat_axis=0, tiled=True),
        lax.all_to_all(keys, "head", split_axis=1, concat_axis=0, tiled=True),
        lax.all_to_all(values, "head", split_axis=1, concat_axis=0, tiled=True),
        lax.all_to_all(out_grad, "head", split_axis=1, concat_axis=0, tiled=True),
    )
    key_every, value_every = (
        lax.all_gather(key_here, "seq", axis=0, tiled=True),
        lax.all_gather(value_here, "seq", axis=0, tiled=True),
    )
    local_rows = query_here.shape[0]
    per_group = local_rows // BLOCK
    heads_here = query_here.shape[1] // HD
    total_rows = key_every.shape[0]
    block_count = total_rows // BLOCK
    first_block = lax.axis_index("seq") * per_group
    item_count = heads_here * per_group

    def one_item(item_index):
        head_slot = item_index // per_group
        block_slot = item_index % per_group
        block_id = first_block + block_slot
        chosen = lax.dynamic_slice(selected, (head_slot, block_slot, 0), (1, 1, TOP)).reshape(TOP)
        block_list = jnp.concatenate([chosen, block_id[None]])
        column = head_slot * HD
        query_rows = lax.dynamic_slice(query_here, (block_slot * BLOCK, column), (BLOCK, HD))
        grad_rows = lax.dynamic_slice(grad_here, (block_slot * BLOCK, column), (BLOCK, HD))
        key_set = jnp.concatenate(
            [
                lax.dynamic_slice(key_every, (block_list[slot] * BLOCK, column), (BLOCK, HD))
                for slot in range(TOP + 1)
            ],
            0,
        )
        value_set = jnp.concatenate(
            [
                lax.dynamic_slice(value_every, (block_list[slot] * BLOCK, column), (BLOCK, HD))
                for slot in range(TOP + 1)
            ],
            0,
        )
        live_rows = block_id * BLOCK + jnp.arange(BLOCK, dtype=jnp.int32) < length[0]
        output, query_grad, key_term, value_term = attend(
            query_rows,
            key_set,
            value_set,
            grad_rows,
            usable_mask(chosen, block_id, BLOCK),
            live_rows,
        )
        return (output, query_grad, key_term, value_term, block_list)

    outputs, query_grads, key_terms, value_terms, owners = lax.map(
        one_item, jnp.arange(item_count, dtype=jnp.int32)
    )

    def to_local(stacked):
        return (
            stacked.reshape(heads_here, per_group, BLOCK, HD)
            .transpose(1, 2, 0, 3)
            .reshape(local_rows, heads_here * HD)
        )

    attended, query_grad = (
        lax.all_to_all(to_local(outputs), "head", split_axis=0, concat_axis=1, tiled=True),
        lax.all_to_all(to_local(query_grads), "head", split_axis=0, concat_axis=1, tiled=True),
    )
    block_ids = owners.reshape(heads_here, per_group * (TOP + 1))
    onehot = (
        jnp.arange(block_count, dtype=jnp.int32)[None, :, None] == block_ids[:, None, :]
    ).astype(jnp.float32)

    def spread(terms):
        grouped = terms.reshape(heads_here, per_group * (TOP + 1), BLOCK, HD)
        summed = jnp.einsum("hke,herd->krhd", onehot, grouped, precision=lax.Precision.HIGHEST)
        return summed.reshape(total_rows, heads_here * HD).astype(jnp.bfloat16)

    key_partial = spread(key_terms)
    value_partial = spread(value_terms)
    stacked = jnp.concatenate([key_partial, value_partial], 1)
    summed = lax.psum_scatter(
        stacked.astype(jnp.float32).astype(jnp.bfloat16), "seq", scatter_dimension=0, tiled=True
    )
    column_count = key_partial.shape[1]
    key_grad, value_grad = (
        lax.all_to_all(summed[:, :column_count], "head", split_axis=0, concat_axis=1, tiled=True),
        lax.all_to_all(summed[:, column_count:], "head", split_axis=0, concat_axis=1, tiled=True),
    )
    return (attended, query_grad, key_grad, value_grad)


def solution(mesh):
    placed = (
        P(("seq", "head"), None),
        P(("seq", "head"), None),
        P(("seq", "head"), None),
        P(("seq", "head"), None),
        P("head", "seq", None),
        P(),
    )
    return jax.shard_map(
        body,
        mesh=mesh,
        in_specs=placed,
        out_specs=(
            P(("seq", "head"), None),
            P(("seq", "head"), None),
            P(("seq", "head"), None),
            P(("seq", "head"), None),
        ),
        check_vma=False,
    )
```

profile of v0, /device:TPU:1, one launch (start us, length us, event | category | flops | bytes accessed | tf_op | source)
XLA Modules:
  0.0 635.5 jit_solution(4688856832204279805)
XLA Ops:
  8.4 26.9 %all_to_all.152 = bf16[32,32,256]{2,0,1:T(8,128)(2,1)} all-to-all(bf16[32,32,256]{2,0,1:T(8,128)(2,1)S(1)} %bitcast.142), channel_id=1, replica_groups=mesh['seq'=8,'head'=32] {'head'}, dimensions={1} | all-to-all | bytes 1048576 | tf_op jit(solution)/shard_map/all_to_all | solution.py:47
  36.5 31.6 %all_to_all.153 = bf16[32,32,256]{2,0,1:T(8,128)(2,1)} all-to-all(bf16[32,32,256]{2,0,1:T(8,128)(2,1)S(1)} %bitcast.143), channel_id=1, replica_groups=mesh['seq'=8,'head'=32] {'head'}, dimensions={1} | all-to-all | bytes 1048576 | tf_op jit(solution)/shard_map/all_to_all | solution.py:48
  69.0 3.7 all-to-all-start
  73.5 54.0 %all-to-all-done = bf16[32,32,256]{2,0,1:T(8,128)(2,1)S(1)} async-done(((bf16[32,32,256]{2,0,1:T(8,128)(2,1)}), bf16[32,32,256]{2,0,1:T(8,128)(2,1)S(1)}, u32[]{:S(2)}, u32[]{:S(2)}) %all-to-all-start) | async-done | bytes 524320 | tf_op jit(solution)/shard_map/all_to_all | solution.py:46
  127.5 3.8 all-to-all-start.3
  131.4 16.8 %all-to-all-done.3 = bf16[32,32,256]{2,0,1:T(8,128)(2,1)S(1)} async-done(((bf16[32,32,256]{2,0,1:T(8,128)(2,1)}), bf16[32,32,256]{2,0,1:T(8,128)(2,1)S(1)}, u32[]{:S(2)}, u32[]{:S(2)}) %all-to-all-start.3) | async-done | bytes 524320 | tf_op jit(solution)/shard_map/all_to_all | solution.py:49
  148.2 100.4 %all-gather.5.cloned.1.call-done = bf16[8192,256]{1,0:T(8,128)(2,1)} async-done(((bf16[1024,256]{1,0:T(8,128)(2,1)}), bf16[8192,256]{1,0:T(8,128)(2,1)}) %all-gather.5.cloned.1.call-update) | async-done | bytes 4194320 | tf_op jit(solution)/shard_map/all_gather | solution.py:53
  248.6 90.3 %while.20 = (s32[]{:T(128)}, bf16[4,512,128]{1,2,0:T(8,128)(2,1)S(1)}, bf16[4,512,128]{2,1,0:T(8,128)(2,1)S(1)}, f32[4,2048,128]{2,1,0:T(8,128)}, f32[4,2048,128...) while((s32[]{:T(128)}, ...), condition=%wide.region_4.5_spmd, body=%wide.region_0.4_spmd.sunk | while | flops 1638792704 | bytes 69374464 | solution.py:97
  257.6 1.9 copy-done
  261.1 4.5 fusion.62
  268.6 1.8 fusion.61
  280.3 1.9 copy-done
  283.7 4.4 fusion.62
  302.8 1.9 copy-done
  306.3 4.4 fusion.62
  325.3 1.9 copy-done
  328.8 4.4 fusion.62
  338.9 9.7 %convert_bitcast_fusion.1 = bf16[16,512,2,128]{3,0,1,2:T(8,128)(2,1)} fusion(f32[2,8,512,128]{3,2,1,0:T(8,128)} %bitcast.130, s32[2,8]{1,0:T(2,128)S(1)} %eq.20), kind=kOutput, calls=%fused_computation.42 | convolution fusion | flops 203424000 | bytes 8388672 | tf_op jit(solution)/shard_map/hke,herd->krhd/dot_general | solution.py:119
  348.6 8.6 %copy.59 = bf16[16,512,2,128]{1,0,3,2:T(8,128)(2,1)} copy(bf16[16,512,2,128]{3,0,1,2:T(8,128)(2,1)} %convert_bitcast_fusion.1) | data formatting | bytes 8388608 | tf_op jit(solution)/shard_map/convert_element_type | solution.py:120
  357.2 8.6 %copy.76 = bf16[32,8,16,512]{3,1,2,0:T(8,128)(2,1)} copy(bf16[32,8,16,512]{3,2,1,0:T(8,128)(2,1)} %bitcast.126) | data formatting | bytes 8388608
  365.9 6.4 %convert_bitcast_fusion = bf16[16,512,2,128]{3,0,1,2:T(8,128)(2,1)} fusion(f32[2,8,512,128]{3,2,1,0:T(8,128)S(1)} %bitcast.131, s32[2,8]{1,0:T(2,128)S(1)} %eq.20), kind=kOutput, calls=%fused_computation.41 | convolution fusion | flops 203424000 | bytes 8388672 | tf_op jit(solution)/shard_map/hke,herd->krhd/dot_general | solution.py:119
  372.3 8.6 %copy.61 = bf16[16,512,2,128]{1,0,3,2:T(8,128)(2,1)} copy(bf16[16,512,2,128]{3,0,1,2:T(8,128)(2,1)} %convert_bitcast_fusion) | data formatting | bytes 8388608 | tf_op jit(solution)/shard_map/convert_element_type | solution.py:120
  380.9 8.4 %copy.77 = bf16[32,8,16,512]{3,1,2,0:T(8,128)(2,1)} copy(bf16[32,8,16,512]{3,2,1,0:T(8,128)(2,1)} %bitcast.127) | data formatting | bytes 8388608
  389.3 7.7 %pad_maximum_fusion.6 = bf16[8192,512]{0,1:T(8,128)(2,1)} fusion(bf16[8192,256]{0,1:T(8,128)(2,1)} %bitcast.129, bf16[8192,256]{0,1:T(8,128)(2,1)} %bitcast.128), kind=kLoop, calls=%fused_computation.36 | loop fusion | flops 16777216 | bytes 16777216 | tf_op jit(solution)/shard_map/concatenate | solution.py:124
  398.6 5.9 all-to-all-start.4
  406.1 38.5 %all-to-all-done.4 = bf16[32,32,256]{2,1,0:T(8,128)(2,1)S(1)} async-done(((bf16[32,32,256]{2,1,0:T(8,128)(2,1)}), bf16[32,32,256]{2,1,0:T(8,128)(2,1)S(1)}, u32[]{:S(2)}, u32[]{:S(2)}) %all-to-all-start.4) | async-done | bytes 524320 | tf_op jit(solution)/shard_map/all_to_all | solution.py:109
  444.6 3.7 all-to-all-start.5
  448.3 132.2 %reduce-scatter.2.cloned.1.call-done = bf16[1024,512]{0,1:T(8,128)(2,1)} async-done(((bf16[8192,512]{0,1:T(8,128)(2,1)}), bf16[1024,512]{0,1:T(8,128)(2,1)}) %reduce-scatter.2.cloned.1.call-update) | async-done | bytes 1048592 | tf_op jit(solution)/shard_map/reduce_scatter | solution.py:125
  582.7 8.1 %all-to-all-start.6 = ((bf16[32,32,256]{2,1,0:T(8,128)(2,1)}), bf16[32,32,256]{2,1,0:T(8,128)(2,1)S(1)}, u32[]{:S(2)}, u32[]{:S(2)}) async-start(bf16[32,32,256]{2,1,0:T(8,128)(2,1)} %bitcast.33), calls=%async_computation.7 | async-start | bytes 1048576 | tf_op jit(solution)/shard_map/all_to_all | solution.py:130
  591.9 15.8 %all-to-all-done.6 = bf16[32,32,256]{2,1,0:T(8,128)(2,1)S(1)} async-done(((bf16[32,32,256]{2,1,0:T(8,128)(2,1)}), bf16[32,32,256]{2,1,0:T(8,128)(2,1)S(1)}, u32[]{:S(2)}, u32[]{:S(2)}) %all-to-all-start.6) | async-done | bytes 524320 | tf_op jit(solution)/shard_map/all_to_all | solution.py:130
  607.7 3.7 all-to-all-start.7
  613.8 14.3 %all-to-all-done.7 = bf16[32,32,256]{2,1,0:T(8,128)(2,1)S(1)} async-done(((bf16[32,32,256]{2,1,0:T(8,128)(2,1)}), bf16[32,32,256]{2,1,0:T(8,128)(2,1)S(1)}, u32[]{:S(2)}, u32[]{:S(2)}) %all-to-all-start.7) | async-done | bytes 524320 | tf_op jit(solution)/shard_map/all_to_all | solution.py:131
  (127 shorter events, 58.5 us)
Async XLA Ops:
  7.2 60.9 %copy-start.3 = (bf16[32,8192]{1,0:T(8,128)(2,1)S(1)}, bf16[32,8192]{1,0:T(8,128)(2,1)}, u32[]{:S(2)}) copy-start(bf16[32,8192]{1,0:T(8,128)(2,1)} %param.8) | copy-start | bytes 1572868
  7.2 65.5 %copy-start.4 = (bf16[32,8192]{1,0:T(8,128)(2,1)S(1)}, bf16[32,8192]{1,0:T(8,128)(2,1)}, u32[]{:S(2)}) copy-start(bf16[32,8192]{1,0:T(8,128)(2,1)} %param.11) | copy-start | bytes 1572868
  7.2 141.0 %all-gather.3.cloned.1.call-start = ((), (), s32[]{:S(2)}) async-start(), calls=%async_computation.9 | async-start | bytes 4718592 | tf_op jit(solution)/shard_map/all_gather | solution.py:52
  35.3 213.3 %all-gather.5.cloned.1.call-start = ((), (), s32[]{:S(2)}) async-start(), calls=%async_computation.10 | async-start | bytes 4718592 | tf_op jit(solution)/shard_map/all_gather | solution.py:53
  69.0 58.5 %all-to-all-start = ((bf16[32,32,256]{2,0,1:T(8,128)(2,1)}), bf16[32,32,256]{2,0,1:T(8,128)(2,1)S(1)}, u32[]{:S(2)}, u32[]{:S(2)}) async-start(bf16[32,32,256]{2,0,1:T(8,128)(2,1)} %bitcast.94), calls=%async_computation | async-start | bytes 1048576 | tf_op jit(solution)/shard_map/all_to_all | solution.py:46
  127.5 20.7 %all-to-all-start.3 = ((bf16[32,32,256]{2,0,1:T(8,128)(2,1)}), bf16[32,32,256]{2,0,1:T(8,128)(2,1)S(1)}, u32[]{:S(2)}, u32[]{:S(2)}) async-start(bf16[32,32,256]{2,0,1:T(8,128)(2,1)} %bitcast.91), calls=%async_computation.3 | async-start | bytes 1048576 | tf_op jit(solution)/shard_map/all_to_all | solution.py:49
  131.3 449.2 %reduce-scatter.2.cloned.1.call-start = ((), (), s32[]{:S(2)}) async-start(), calls=%async_computation.11 | async-start | bytes 9437184 | tf_op jit(solution)/shard_map/reduce_scatter | solution.py:125
  257.6 1.9 copy-start
  261.1 4.5 copy-start.1
  280.3 1.9 copy-start
  283.7 4.4 copy-start.1
  302.8 1.9 copy-start
  306.3 4.4 copy-start.1
  325.3 1.9 copy-start
  328.8 4.4 copy-start.1
  357.2 8.6 %copy-start.2 = (f32[4,2048,128]{2,1,0:T(8,128)S(1)}, f32[4,2048,128]{2,1,0:T(8,128)}, u32[]{:S(2)}) copy-start(f32[4,2048,128]{2,1,0:T(8,128)} %get-tuple-element.188) | copy-start | bytes 12582916
  398.6 46.1 %all-to-all-start.4 = ((bf16[32,32,256]{2,1,0:T(8,128)(2,1)}), bf16[32,32,256]{2,1,0:T(8,128)(2,1)S(1)}, u32[]{:S(2)}, u32[]{:S(2)}) async-start(bf16[32,32,256]{2,1,0:T(8,128)(2,1)} %all_to_all.128), calls=%async_computation.4 | async-start | bytes 1048576 | tf_op jit(solution)/shard_map/all_to_all | solution.py:109
  444.6 138.1 %all-to-all-start.5 = ((bf16[32,32,256]{2,1,0:T(8,128)(2,1)}), bf16[32,32,256]{2,1,0:T(8,128)(2,1)S(1)}, u32[]{:S(2)}, u32[]{:S(2)}) async-start(bf16[32,32,256]{2,1,0:T(8,128)(2,1)} %all_to_all.132), calls=%async_computation.5 | async-start | bytes 1048576 | tf_op jit(solution)/shard_map/all_to_all | solution.py:110
  582.7 24.9 %all-to-all-start.6 = ((bf16[32,32,256]{2,1,0:T(8,128)(2,1)}), bf16[32,32,256]{2,1,0:T(8,128)(2,1)S(1)}, u32[]{:S(2)}, u32[]{:S(2)}) async-start(bf16[32,32,256]{2,1,0:T(8,128)(2,1)} %bitcast.33), calls=%async_computation.7 | async-start | bytes 1048576 | tf_op jit(solution)/shard_map/all_to_all | solution.py:130
  607.7 20.5 %all-to-all-start.7 = ((bf16[32,32,256]{2,1,0:T(8,128)(2,1)}), bf16[32,32,256]{2,1,0:T(8,128)(2,1)S(1)}, u32[]{:S(2)}, u32[]{:S(2)}) async-start(bf16[32,32,256]{2,1,0:T(8,128)(2,1)} %bitcast.35), calls=%async_computation.8 | async-start | bytes 1048576 | tf_op jit(solution)/shard_map/all_to_all | solution.py:131
Sparse Core Ops, SparseCore 0:
  35.4 94.9 all-gather.2
  133.1 115.4 all-gather.4
  397.1 183.2 reduce-scatter.1
where the time goes:
time: 637 us; the launch traced here: 636 us
  waiting for transfers between devices  372 us (58%)
  local copies, waits for them, and re-layouts  67.5 us (11%)
  matrix products  59.3 us (9%)
  blocking collectives  58.5 us (9%)
  starting transfers between devices  28.9 us (5%)
  loops' own time  18.5 us (3%)
  other arithmetic  16.8 us (3%)
  between operations  13.9 us (2%)
    reduce_scatter x1, waiting for transfers between devices, body(): lax.psum_scatter(stacked.astype(jnp.float32).astype(jnp.bfloat16), 'seq',...  132 us
    all_gather x1, waiting for transfers between devices, body(): lax.all_gather(value_here, 'seq', axis=0, tiled=True)  100 us
    all_to_all x1, waiting for transfers between devices, body(): lax.all_to_all(queries, 'head', split_axis=1, concat_axis=0, tiled=True)  54 us
    all_to_all x1, waiting for transfers between devices, body(): lax.all_to_all(to_local(outputs), 'head', split_axis=0, concat_axis=1, ti...  38.5 us
    all_to_all x1, blocking collectives, body(): lax.all_to_all(values, 'head', split_axis=1, concat_axis=0, tiled=True)  31.6 us
    all_to_all x1, blocking collectives, body(): lax.all_to_all(keys, 'head', split_axis=1, concat_axis=0, tiled=True)  26.9 us
    another operation x1, loops' own time, body(): lax.map(one_item, jnp.arange(item_count, dtype=jnp.int32))  18.5 us
    dot_general x4, matrix products, attend(): jnp.dot(weights_low.T, grad_in, preferred_element_type=jnp.float32)  17.7 us
  transfers between devices with their start and end apart: 9, of which 7 were waited for; matrix products, arithmetic and copies ran while one was open for 2% of the time, Pallas kernels for 0%

commit v1 on v0

v1 whole, which is shorter than its diff:
```python
import math

import jax
import jax.numpy as jnp
from jax import lax
from jax.experimental import pallas as pl
from jax.experimental.pallas import tpu as pltpu
from jax.sharding import PartitionSpec as P

HD = 128
BLOCK = 512
TOP = 3
ROWS = 32
HEADS = 64
QUARTER = 2048
TOKENS = 8192
PEERS = 64

NEG = -1e30
SCALE = 1.0 / math.sqrt(HD)
SCALE2 = SCALE * math.log2(math.e)


def place():
    s = lax.axis_index("seq")
    hh = lax.axis_index("head")
    zh, x = lax.div(s, 4), lax.rem(s, 4)
    yz, c = lax.div(hh, 2), lax.rem(hh, 2)
    half = lax.div(x, 2)
    pair = jnp.where(half == 0, x, 3 - x)
    return s, hh, zh, x, yz, c, half, pair


def dev(s, hh):
    return {"seq": s, "head": hh}


def head_holder(h, half, zh):
    pair = lax.rem(lax.div(h, 2), 2)
    x = jnp.where(half == 0, pair, 3 - pair)
    return dev(lax.rem(h, 2) * 4 + x, lax.div(h, 4) * 2 + zh)


def greet(s, hh, zh, x, yz, c, half):
    barrier = pltpu.get_barrier_semaphore()
    mine = h_of()
    own = c == zh

    def to_holder(i, carry):
        @pl.when(jnp.logical_not(jnp.logical_and(own, i == 0)))
        def _():
            pl.semaphore_signal(barrier, inc=1, device_id=head_holder(lax.rem(mine + i, HEADS), half, zh))
        return carry

    def to_owner(i, carry):
        r = lax.rem(lax.rem(x, 2) * 32 + hh + i, PEERS)

        @pl.when(jnp.logical_not(jnp.logical_and(own, i == 0)))
        def _():
            pl.semaphore_signal(barrier, inc=1, device_id=owner_of(r, half, c))
        return carry

    return barrier, to_holder, to_owner


def h_of():
    s, hh, zh, x, yz, c, half, pair = place()
    return 2 * (yz * 2 + pair) + zh


def owner_of(r, half, c):
    return dev(c * 4 + 2 * half + lax.div(r, 32), lax.rem(r, 32))


def mates(s, hh, zh, x, yz, c):
    across = zh * 4 + 3 - x
    return dev(across, hh), dev(s, yz * 2 + 1 - c), dev(across, yz * 2 + 1 - c)


def whole_wait(ref, sem):
    pltpu.make_async_copy(ref, ref, sem).wait()


def gather_kernel(k_ref, v_ref, q_ref, g_ref, sel_ref, k_out, v_out, q_out, g_out, sel_out,
                  own_sem, arrive, left, pass_arrive, pass_left, sel_sem):
    s, hh, zh, x, yz, c, half, pair = place()
    mine = h_of()
    own = c == zh
    barrier, _, to_owner = greet(s, hh, zh, x, yz, c, half)
    lax.fori_loop(0, PEERS, to_owner, 0)
    across, beside, diagonal = mates(s, hh, zh, x, yz, c)
    for mate in (across, beside, diagonal):
        pl.semaphore_signal(barrier, inc=1, device_id=mate)
    pl.semaphore_wait(barrier, PEERS + 3 - own.astype(jnp.int32))

    row_quarter = (lax.rem(x, 2) * 32 + hh) * ROWS
    row_all = (s * 32 + hh) * ROWS

    def scatter(n, src, dst, row):
        row = pl.multiple_of(row, ROWS)

        def one(i, carry):
            h = lax.rem(mine + i, HEADS)
            part = src.at[:, pl.ds(pl.multiple_of(h * HD, HD), HD)]
            there = dst.at[pl.ds(row, ROWS), :]
            keep = jnp.logical_and(own, i == 0)

            @pl.when(keep)
            def _():
                pltpu.make_async_copy(part, there, arrive.at[n]).start()

            @pl.when(jnp.logical_not(keep))
            def _():
                pltpu.make_async_remote_copy(part, there, left.at[n], arrive.at[n],
                                             device_id=head_holder(h, half, zh)).start()
            return carry
        lax.fori_loop(0, PEERS, one, 0)

    for hb in range(2):
        h = 2 * (yz * 2 + c) + hb
        keep = jnp.logical_and(own, jnp.logical_and(hb == zh, c == pair))
        there = sel_out.at[lax.rem(x, 2)]

        @pl.when(keep)
        def _(hb=hb, there=there):
            pltpu.make_async_copy(sel_ref.at[hb], there, sel_sem.at[0]).start()

        @pl.when(jnp.logical_not(keep))
        def _(hb=hb, there=there, h=h):
            pltpu.make_async_remote_copy(sel_ref.at[hb], there, sel_sem.at[1], sel_sem.at[0],
                                         device_id=head_holder(h, half, zh)).start()

    scatter(0, k_ref, k_out, row_all)
    scatter(1, v_ref, v_out, row_all)

    q = c * 2 + half
    outs = (k_out, v_out)

    def region(a, p):
        return outs[a].at[pl.ds(p * QUARTER, QUARTER), :]

    def hand_on(a, p, slot, target):
        return pltpu.make_async_remote_copy(region(a, p), region(a, p), pass_left.at[a, slot],
                                            pass_arrive.at[a, p], device_id=target)

    def quarter_rows(a):
        return outs[a].at[pl.ds(pl.multiple_of(q * QUARTER, QUARTER), QUARTER), :]

    for a in range(2):
        whole_wait(quarter_rows(a), arrive.at[a])

        @pl.when(q == 0)
        def _(a=a):
            hand_on(a, 0, 0, across).start()
            hand_on(a, 0, 1, beside).start()

        @pl.when(q == 1)
        def _(a=a):
            hand_on(a, 1, 0, diagonal).start()
            hand_on(a, 1, 1, beside).start()

        @pl.when(q == 2)
        def _(a=a):
            hand_on(a, 2, 0, across).start()

        if a == 0:
            scatter(2, q_ref, q_out, row_quarter)
            scatter(3, g_ref, g_out, row_quarter)

    for a in range(2):
        @pl.when(q == 1)
        def _(a=a):
            whole_wait(region(a, 0), pass_arrive.at[a, 0])
            hand_on(a, 0, 2, beside).start()

    for a in range(2):
        @pl.when(q >= 2)
        def _(a=a):
            whole_wait(region(a, 0), pass_arrive.at[a, 0])
            whole_wait(region(a, 1), pass_arrive.at[a, 1])

        @pl.when(q == 3)
        def _(a=a):
            whole_wait(region(a, 2), pass_arrive.at[a, 2])
    whole_wait(q_out, arrive.at[2])
    whole_wait(g_out, arrive.at[3])
    whole_wait(sel_out, sel_sem.at[0])

    for a in range(2):
        @pl.when(q == 0)
        def _(a=a):
            whole_wait(region(a, 0), pass_left.at[a, 0])
            whole_wait(region(a, 0), pass_left.at[a, 1])

        @pl.when(q == 1)
        def _(a=a):
            whole_wait(region(a, 1), pass_left.at[a, 0])
            whole_wait(region(a, 1), pass_left.at[a, 1])
            whole_wait(region(a, 0), pass_left.at[a, 2])

        @pl.when(q == 2)
        def _(a=a):
            whole_wait(region(a, 2), pass_left.at[a, 0])
    part = q_out.at[pl.ds(0, QUARTER - ROWS), :]
    last = q_out.at[pl.ds(0, ROWS), :]
    for n in range(4):
        whole_wait(part, left.at[n])

        @pl.when(jnp.logical_not(own))
        def _(n=n):
            whole_wait(last, left.at[n])
    for hb in range(2):
        keep = jnp.logical_and(own, jnp.logical_and(hb == zh, c == pair))

        @pl.when(jnp.logical_not(keep))
        def _(hb=hb):
            whole_wait(sel_ref.at[hb], sel_sem.at[1])


def attend_kernel(sel_ref, info_ref, q_ref, g_ref, k_ref, v_ref, o_ref, dq_ref, dk_ref, dv_ref,
                  dk_acc, dv_acc, st):
    first = info_ref[0]
    length = info_ref[1]
    dk_acc[...] = jnp.zeros_like(dk_acc)
    dv_acc[...] = jnp.zeros_like(dv_acc)
    nt = (((1,), (1,)), ((), ()))
    tn = (((0,), (0,)), ((), ()))

    def rows_of(block):
        return pl.ds(pl.multiple_of(block * BLOCK, BLOCK), BLOCK)

    def one_block(j, carry):
        b = first + j
        rows = rows_of(j)
        q = q_ref[rows, :]
        live = (b * BLOCK + lax.broadcasted_iota(jnp.int32, (BLOCK, 1), 0)) < length
        g = jnp.where(live, g_ref[rows, :], jnp.zeros((), jnp.bfloat16))
        slot_rows = lax.div(j, 2)
        lane = lax.rem(j, 2) * TOP
        ids = [sel_ref[slot_rows, 0, lane + t] for t in range(TOP)] + [b]
        m = jnp.full((1, BLOCK), NEG, jnp.float32)
        for t in range(TOP + 1):
            sc = lax.dot_general(k_ref[rows_of(ids[t]), :], q, nt, preferred_element_type=jnp.float32)
            if t < TOP:
                sc = jnp.where(ids[t] < b, sc, NEG)
            else:
                kv = lax.broadcasted_iota(jnp.int32, (BLOCK, BLOCK), 0)
                qp = lax.broadcasted_iota(jnp.int32, (BLOCK, BLOCK), 1)
                sc = jnp.where(kv <= qp, sc, NEG)
            st[t] = sc
            m = jnp.maximum(m, jnp.max(sc, axis=0, keepdims=True))
        total = jnp.zeros((1, BLOCK), jnp.float32)
        for t in range(TOP + 1):
            p = jnp.exp2((st[t] - m) * SCALE2)
            total = total + jnp.sum(p, axis=0, keepdims=True)
            st[t] = p
        inv = 1.0 / total
        out_t = jnp.zeros((HD, BLOCK), jnp.float32)
        for t in range(TOP + 1):
            w = st[t] * inv
            st[t] = w
            low = w.astype(jnp.bfloat16)
            out_t = out_t + lax.dot_general(v_ref[rows_of(ids[t]), :], low, tn, preferred_element_type=jnp.float32)
            dv_acc[rows_of(ids[t]), :] += jnp.dot(low, g, preferred_element_type=jnp.float32)
        out = jnp.where(live, out_t.T, 0.0).astype(jnp.bfloat16)
        o_ref[rows, :] = out
        delta = jnp.sum((g.astype(jnp.float32) * out.astype(jnp.float32)).T, axis=0, keepdims=True)
        dq_t = jnp.zeros((HD, BLOCK), jnp.float32)
        for t in range(TOP + 1):
            dw = lax.dot_general(v_ref[rows_of(ids[t]), :], g, nt, preferred_element_type=jnp.float32)
            ds = (st[t] * (dw - delta) * SCALE).astype(jnp.bfloat16)
            dq_t = dq_t + lax.dot_general(k_ref[rows_of(ids[t]), :], ds, tn, preferred_element_type=jnp.float32)
            dk_acc[rows_of(ids[t]), :] += jnp.dot(ds, q, preferred_element_type=jnp.float32)
        dq_ref[rows, :] = dq_t.T.astype(jnp.bfloat16)
        return carry

    lax.fori_loop(0, QUARTER // BLOCK, one_block, 0)
    dk_ref[...] = dk_acc[...].astype(jnp.bfloat16)
    dv_ref[...] = dv_acc[...].astype(jnp.bfloat16)


def return_kernel(o_ref, dq_ref, dk_ref, dv_ref, o_out, dq_out, dk_out, dv_out,
                  own_part, near_part, got, relay, final, load_sem,
                  arrive, left, part_arrive, part_left):
    s, hh, zh, x, yz, c, half, pair = place()
    mine = h_of()
    own = c == zh
    q = c * 2 + half
    barrier, to_holder, _ = greet(s, hh, zh, x, yz, c, half)
    lax.fori_loop(0, PEERS, to_holder, 0)
    across, beside, diagonal = mates(s, hh, zh, x, yz, c)
    for mate in (across, beside, diagonal):
        pl.semaphore_signal(barrier, inc=1, device_id=mate)

    parts = (dk_ref, dv_ref)

    def region(a, p):
        return parts[a].at[pl.ds(pl.multiple_of(p * QUARTER, QUARTER), QUARTER), :]

    for a in range(2):
        pltpu.make_async_copy(region(a, q), own_part.at[a], load_sem.at[a]).start()

        @pl.when(q == 1)
        def _(a=a):
            pltpu.make_async_copy(region(a, 0), near_part.at[a], load_sem.at[2 + a]).start()

    pl.semaphore_wait(barrier, PEERS + 3 - own.astype(jnp.int32))

    def send_part(a, p, slot, into, target):
        return pltpu.make_async_remote_copy(region(a, p), got.at[a, into], part_left.at[a, slot],
                                            part_arrive.at[a, into], device_id=target)

    for a in range(2):
        @pl.when(q == 3)
        def _(a=a):
            send_part(a, 0, 0, 2, beside).start()
            send_part(a, 1, 1, 1, beside).start()
            send_part(a, 2, 2, 0, across).start()

        @pl.when(q == 2)
        def _(a=a):
            send_part(a, 0, 0, 1, beside).start()
            send_part(a, 1, 1, 0, diagonal).start()

    start_row = lax.rem(x, 2) * 32 + hh
    column = pl.ds(pl.multiple_of(mine * HD, HD), HD)

    def scatter(n, src, dst):
        def one(i, carry):
            r = lax.rem(start_row + i, PEERS)
            part = src.at[pl.ds(pl.multiple_of(r * ROWS, ROWS), ROWS), :]
            there = dst.at[:, column]
            keep = jnp.logical_and(own, i == 0)

            @pl.when(keep)
            def _():
                pltpu.make_async_copy(part, there, arrive.at[n]).start()

            @pl.when(jnp.logical_not(keep))
            def _():
                pltpu.make_async_remote_copy(part, there, left.at[n], arrive.at[n],
                                             device_id=owner_of(r, half, c)).start()
            return carry
        lax.fori_loop(0, PEERS, one, 0)

    def relay_copy(a):
        return pltpu.make_async_remote_copy(relay.at[a], got.at[a, 0], part_left.at[a, 0],
                                            part_arrive.at[a, 0], device_id=across)

    scatter(0, o_ref, o_out)

    @pl.when(q == 1)
    def _():
        for a in range(2):
            pltpu.make_async_copy(region(a, 0), near_part.at[a], load_sem.at[2 + a]).wait()
            whole_wait(got.at[a, 2], part_arrive.at[a, 2])
            relay[a] = (near_part[a].astype(jnp.float32) + got[a, 2].astype(jnp.float32)).astype(jnp.bfloat16)
            relay_copy(a).start()

    scatter(1, dq_ref, dq_out)

    for a in range(2):
        pltpu.make_async_copy(region(a, q), own_part.at[a], load_sem.at[a]).wait()

        @pl.when(q < 2)
        def _(a=a):
            whole_wait(got.at[a, 0], part_arrive.at[a, 0])
            whole_wait(got.at[a, 1], part_arrive.at[a, 1])
            final[a] = (own_part[a].astype(jnp.float32) + got[a, 0].astype(jnp.float32)
                        + got[a, 1].astype(jnp.float32)).astype(jnp.bfloat16)

        @pl.when(q == 2)
        def _(a=a):
            whole_wait(got.at[a, 0], part_arrive.at[a, 0])
            final[a] = (own_part[a].astype(jnp.float32) + got[a, 0].astype(jnp.float32)).astype(jnp.bfloat16)

        @pl.when(q == 3)
        def _(a=a):
            final[a] = own_part[a]
        scatter(2 + a, final.at[a], dk_out if a == 0 else dv_out)

    for n, out in enumerate((o_out, dq_out, dk_out, dv_out)):
        whole_wait(out, arrive.at[n])
    for a in range(2):
        @pl.when(q == 3)
        def _(a=a):
            for slot in range(3):
                whole_wait(got.at[a, 0], part_left.at[a, slot])

        @pl.when(q == 2)
        def _(a=a):
            for slot in range(2):
                whole_wait(got.at[a, 0], part_left.at[a, slot])

        @pl.when(q == 1)
        def _(a=a):
            whole_wait(got.at[a, 0], part_left.at[a, 0])
    part = final.at[0, pl.ds(0, QUARTER - ROWS), :]
    last = final.at[0, pl.ds(0, ROWS), :]
    for n in range(4):
        whole_wait(part, left.at[n])

        @pl.when(jnp.logical_not(own))
        def _(n=n):
            whole_wait(last, left.at[n])


ANY = pl.BlockSpec(memory_space=pl.ANY)
VMEM = pl.BlockSpec(memory_space=pltpu.VMEM)
SMEM = pl.BlockSpec(memory_space=pltpu.SMEM)


def body(queries, keys, values, out_grad, selected, length):
    low = jnp.bfloat16
    shape = jax.ShapeDtypeStruct
    dma = pltpu.SemaphoreType.DMA
    padded = jnp.pad(selected.reshape(2, 1, 2 * TOP), ((0, 0), (0, 7), (0, 128 - 2 * TOP)))
    k_all, v_all, q_here, g_here, sel = pl.pallas_call(
        gather_kernel,
        out_shape=(shape((TOKENS, HD), low), shape((TOKENS, HD), low), shape((QUARTER, HD), low),
                   shape((QUARTER, HD), low), shape((2, 8, 128), jnp.int32)),
        in_specs=[ANY] * 5,
        out_specs=(ANY,) * 5,
        scratch_shapes=[dma((1,)), dma((4,)), dma((4,)), dma((2, 3)), dma((2, 3)), dma((2,))],
        compiler_params=pltpu.CompilerParams(collective_id=0, has_side_effects=True),
        name="gather",
    )(keys, values, queries, out_grad, padded)

    s, hh, zh, x, yz, c, half, pair = place()
    first = (c * 2 + half) * (QUARTER // BLOCK)
    info = jnp.stack([first, length[0]]).astype(jnp.int32)
    o, dq, dk, dv = pl.pallas_call(
        attend_kernel,
        out_shape=(shape((QUARTER, HD), low), shape((QUARTER, HD), low),
                   shape((TOKENS, HD), low), shape((TOKENS, HD), low)),
        in_specs=[SMEM, SMEM, VMEM, VMEM, VMEM, VMEM],
        out_specs=(VMEM,) * 4,
        scratch_shapes=[pltpu.VMEM((TOKENS, HD), jnp.float32), pltpu.VMEM((TOKENS, HD), jnp.float32),
                        pltpu.VMEM((TOP + 1, BLOCK, BLOCK), jnp.float32)],
        compiler_params=pltpu.CompilerParams(vmem_limit_bytes=60 * 1024 * 1024),
        name="attend",
    )(sel, info, q_here, g_here, k_all, v_all)

    owned = shape((ROWS, HEADS * HD), low)
    return pl.pallas_call(
        return_kernel,
        out_shape=(owned,) * 4,
        in_specs=[ANY] * 4,
        out_specs=(ANY,) * 4,
        scratch_shapes=[pltpu.VMEM((2, QUARTER, HD), low), pltpu.VMEM((2, QUARTER, HD), low),
                        pltpu.VMEM((2, 3, QUARTER, HD), low), pltpu.VMEM((2, QUARTER, HD), low),
                        pltpu.VMEM((2, QUARTER, HD), low), dma((4,)), dma((4,)), dma((4,)),
                        dma((2, 3)), dma((2, 3))],
        compiler_params=pltpu.CompilerParams(collective_id=1, has_side_effects=True,
                                             vmem_limit_bytes=32 * 1024 * 1024),
        name="give_back",
    )(o, dq, dk, dv)


def solution(mesh):
    rows = P(("seq", "head"), None)
    return jax.shard_map(
        body,
        mesh=mesh,
        in_specs=(rows, rows, rows, rows, P("head", "seq", None), P()),
        out_specs=(rows, rows, rows, rows),
        check_vma=False,
    )
```

time: 637 us -> 149 us (0.23)
  waiting for transfers between devices: 372 us -> 0 us
  Pallas kernels: 0 us -> 137 us
  matrix products: 59.3 us -> 0 us
  blocking collectives: 58.5 us -> 0 us
  local copies, waits for them, and re-layouts: 67.5 us -> 9.8 us
  starting transfers between devices: 28.9 us -> 0 us
  loops' own time: 18.5 us -> 0 us
  other arithmetic: 16.8 us -> 0.59 us
  between operations: 13.9 us -> 1.31 us
    all_to_all x6 -> x0, waiting for transfers between devices: 139 us -> none  [the longest x1 54 us: body(): lax.all_to_all(queries, 'head', split_axis=1, concat_axis=0, tiled=True)]
    pallas_call x0 -> x3, Pallas kernels: none -> 137 us  [the longest x1 58.7 us: body(): pl.pallas_call(gather_kernel, out_shape=(shape((TOKENS, HD), low), shape(...]
    reduce_scatter x1 -> x0, waiting for transfers between devices: 132 us -> none  [body(): lax.psum_scatter(stacked.astype(jnp.float32).astype(jnp.bfloat16), 'seq',...]
    all_gather x2 -> x0, waiting for transfers between devices: 100 us -> none  [the longest x1 100 us: body(): lax.all_gather(value_here, 'seq', axis=0, tiled=True)]
    dot_general x26 -> x0, matrix products: 59.3 us -> none  [the longest x4 17.7 us: attend(): jnp.dot(weights_low.T, grad_in, preferred_element_type=jnp.float32)]
    all_to_all x2 -> x0, blocking collectives: 58.5 us -> none  [the longest x1 31.6 us: body(): lax.all_to_all(values, 'head', split_axis=1, concat_axis=0, tiled=True)]
    all_to_all x6 -> x0, starting transfers between devices: 28.8 us -> none  [the longest x1 8.12 us: body(): lax.all_to_all(summed[:, :column_count], 'head', split_axis=0, concat_axi...]
    another operation x1 -> x0, loops' own time: 18.5 us -> none  [body(): lax.map(one_item, jnp.arange(item_count, dtype=jnp.int32))]
  transfers between devices with their start and end apart: 9 -> 0, of which waited for: 7 -> 0; matrix products, arithmetic and copies ran while one was open for 2% -> 0% of each run, Pallas kernels for 0% -> 0%
where the time goes in v1:
time: 149 us; the launch traced here: 148 us
  Pallas kernels  137 us (92%)
  local copies, waits for them, and re-layouts  9.8 us (7%)
    pallas_call x1, Pallas kernels, body(): pl.pallas_call(gather_kernel, out_shape=(shape((TOKENS, HD), low), shape(...  58.7 us
    pallas_call x1, Pallas kernels, body(): pl.pallas_call(return_kernel, out_shape=(owned,) * 4, in_specs=[ANY] * 4,...  55.7 us
    pallas_call x1, Pallas kernels, body(): pl.pallas_call(attend_kernel, out_shape=(shape((QUARTER, HD), low), shape...  22.2 us
    unnamed x12, local copies, waits for them, and re-layouts  8.44 us

profile of v1, /device:TPU:1, one launch (start us, length us, event | category | flops | bytes accessed | tf_op | source)
XLA Modules:
  0.0 148.3 jit_solution(7451422485759041741)
XLA Ops:
  1.3 0.6 pad_add_fusion.info_ref
  1.9 0.8 reshape.11
  2.6 0.6 pad.4.sel_ref
  3.2 58.7 %gather.1 = (bf16[8192,128]{1,0:T(8,128)(2,1)}, bf16[8192,128]{1,0:T(8,128)(2,1)}, bf16[2048,128]{1,0:T(8,128)(2,1)}, bf16[2048,128]{1,0:T(8,128)(2,1)}, s32[2,8,128]{2,1,0:T(8,128)}) custom-call(bf16[32,8192]{1,0:T(8,128)(2,1)} %k_ref.1, bf16[32,8192]{1,0:T(8,128)(2,1)} %v_ref.1, bf16[32,8192]{1,0:T(8,128)(2,1)} %q_ref.1, bf16[32,8192]{1,0:T(8,128)(2,1)} %g_ref.1, ...), custom_call_target="tpu_custom_call" | custom-call | tf_op jit(solution)/shard_map/gather/pallas_call | solution.py:418
  62.0 22.2 %attend.1 = (bf16[2048,128]{1,0:T(8,128)(2,1)}, bf16[2048,128]{1,0:T(8,128)(2,1)}, bf16[8192,128]{1,0:T(8,128)(2,1)}, bf16[8192,128]{1,0:T(8,128)(2,1)}) custom-call(s32[2,8,128]{2,1,0:T(8,128)} %get-tuple-element.13.sel_ref, s32[2]{0:T(128)} %pad_add_fusion.info_ref, bf16[2048,128]{1,0:T(8,128)(2,1)} %get-tuple-element.14.q_ref, ...), custom_call_target="tpu_custom_call" | custom-call | tf_op jit(solution)/shard_map/attend/pallas_call | solution.py:432
  84.1 0.0 copy-start
  84.2 1.6 %copy-done = bf16[8192,128]{1,0:T(8,128)(2,1)S(1)} copy-done((bf16[8192,128]{1,0:T(8,128)(2,1)S(1)}, bf16[8192,128]{1,0:T(8,128)(2,1)}, u32[]{:S(2)}) %copy-start) | copy-done | bytes 2097176
  85.7 0.0 copy-start.1
  85.7 1.6 %copy-done.1 = bf16[8192,128]{1,0:T(8,128)(2,1)S(1)} copy-done((bf16[8192,128]{1,0:T(8,128)(2,1)S(1)}, bf16[8192,128]{1,0:T(8,128)(2,1)}, u32[]{:S(2)}) %copy-start.1) | copy-done | bytes 2097176
  87.3 0.0 copy-start.2
  87.3 1.0 copy-done.2
  88.4 0.0 copy-start.3
  88.4 1.0 copy-done.3
  89.4 55.7 %give_back.1 = (bf16[32,8192]{1,0:T(8,128)(2,1)S(1)}, bf16[32,8192]{1,0:T(8,128)(2,1)S(1)}, bf16[32,8192]{1,0:T(8,128)(2,1)S(1)}, bf16[32,8192]{1,0:T(8,128)(2,1)S(1)}) custom-call(bf16[2048,128]{1,0:T(8,128)(2,1)S(1)} %copy-done.2, bf16[2048,128]{1,0:T(8,128)(2,1)S(1)} %copy-done.3, bf16[8192,128]{1,0:T(8,128)(2,1)S(1)} %copy-done, ...), custom_call_target="tpu_custom_call" | custom-call | tf_op jit(solution)/shard_map/give_back/pallas_call | solution.py:445
  145.2 0.8 copy.16
  146.0 0.8 copy.17
  146.8 0.8 copy.18
  147.5 0.8 copy.19
Async XLA Ops:
  84.1 1.6 %copy-start = (bf16[8192,128]{1,0:T(8,128)(2,1)S(1)}, bf16[8192,128]{1,0:T(8,128)(2,1)}, u32[]{:S(2)}) copy-start(bf16[8192,128]{1,0:T(8,128)(2,1)} %get-tuple-element.20.dk_ref) | copy-start | bytes 6291460
  85.7 1.6 %copy-start.1 = (bf16[8192,128]{1,0:T(8,128)(2,1)S(1)}, bf16[8192,128]{1,0:T(8,128)(2,1)}, u32[]{:S(2)}) copy-start(bf16[8192,128]{1,0:T(8,128)(2,1)} %get-tuple-element.21.dv_ref) | copy-start | bytes 6291460
  87.3 1.0 copy-start.2
  88.4 1.0 copy-start.3

commit v2 on v1

v2 whole, which is shorter than its diff:
```python
import math

import jax
import jax.numpy as jnp
from jax import lax
from jax.experimental import pallas as pl
from jax.experimental.pallas import tpu as pltpu
from jax.sharding import PartitionSpec as P

HD = 128
BLOCK = 512
TOP = 3
ROWS = 32
HEADS = 64
QUARTER = 2048
TOKENS = 8192
PEERS = 64

NEG = -1e30
SCALE = 1.0 / math.sqrt(HD)
SCALE2 = SCALE * math.log2(math.e)


def place():
    s = lax.axis_index("seq")
    hh = lax.axis_index("head")
    zh, x = lax.div(s, 4), lax.rem(s, 4)
    yz, c = lax.div(hh, 2), lax.rem(hh, 2)
    half = lax.div(x, 2)
    pair = jnp.where(half == 0, x, 3 - x)
    return s, hh, zh, x, yz, c, half, pair


def dev(s, hh):
    return {"seq": s, "head": hh}


def head_holder(h, half, zh):
    pair = lax.rem(lax.div(h, 2), 2)
    x = jnp.where(half == 0, pair, 3 - pair)
    return dev(lax.rem(h, 2) * 4 + x, lax.div(h, 4) * 2 + zh)


def h_of():
    s, hh, zh, x, yz, c, half, pair = place()
    return 2 * (yz * 2 + pair) + zh


def owner_of(r, half, c):
    return dev(c * 4 + 2 * half + lax.div(r, 32), lax.rem(r, 32))


def whole_wait(ref, sem):
    pltpu.make_async_copy(ref, ref, sem).wait()


NT = (((1,), (1,)), ((), ()))
TN = (((0,), (0,)), ((), ()))
SLOTS = TOP + 1
NB = QUARTER // BLOCK
NBLK = TOKENS // BLOCK


def fused_kernel(k_ref, v_ref, q_ref, g_ref, chosen_ref, length_ref,
                 o_out, dq_out, dk_out, dv_out,
                 k_all, v_all, q_buf, g_buf, o_buf, dq_buf, sel_own, sel_buf, sel,
                 weights, terms, part, got, relay, final,
                 arrive, left, pass_arrive, pass_left, sel_sem, arrive_out, left_out, part_arrive, part_left):
    s, hh, zh, x, yz, c, half, pair = place()
    mine = h_of()
    own = c == zh
    q = c * 2 + half
    first = q * NB
    across_seq = zh * 4 + 3 - x
    across, beside, diagonal = dev(across_seq, hh), dev(s, yz * 2 + 1 - c), dev(across_seq, yz * 2 + 1 - c)
    start_row = lax.rem(x, 2) * 32 + hh

    barrier = pltpu.get_barrier_semaphore()

    def hello(i, carry):
        r = lax.rem(start_row + i, PEERS)

        @pl.when(jnp.logical_not(jnp.logical_and(own, i == 0)))
        def _():
            pl.semaphore_signal(barrier, inc=1, device_id=owner_of(r, half, c))
        return carry
    lax.fori_loop(0, PEERS, hello, 0)
    for mate in (across, beside, diagonal):
        pl.semaphore_signal(barrier, inc=1, device_id=mate)

    lane = lax.broadcasted_iota(jnp.int32, (8, 128), 1)
    for hb in range(2):
        packed = jnp.zeros((8, 128), jnp.int32)
        for bb in range(2):
            for t in range(TOP):
                packed = jnp.where(lane == bb * TOP + t, chosen_ref[hb, bb, t], packed)
        sel_own[hb] = packed
    pl.semaphore_wait(barrier, PEERS + 3 - own.astype(jnp.int32))

    def scatter(n, src, there):

        def one(i, carry):
            h = lax.rem(mine + i, HEADS)
            piece = src.at[:, pl.ds(pl.multiple_of(h * HD, HD), HD)]
            keep = jnp.logical_and(own, i == 0)

            @pl.when(keep)
            def _():
                pltpu.make_async_copy(piece, there, arrive.at[n]).start()

            @pl.when(jnp.logical_not(keep))
            def _():
                pltpu.make_async_remote_copy(piece, there, left.at[n], arrive.at[n],
                                             device_id=head_holder(h, half, zh)).start()
            return carry
        lax.fori_loop(0, PEERS, one, 0)

    per_block = BLOCK // ROWS
    block_here = 2 * s + lax.div(hh, per_block)
    rows_here = pl.ds(pl.multiple_of(lax.rem(hh, per_block) * ROWS, ROWS), ROWS)
    rows_quarter = pl.ds(pl.multiple_of(start_row * ROWS, ROWS), ROWS)
    scatter(0, k_ref, k_all.at[block_here, rows_here, :])
    scatter(1, v_ref, v_all.at[block_here, rows_here, :])

    def sel_keep(hb):
        return jnp.logical_and(own, jnp.logical_and(hb == zh, c == pair))

    for hb in range(2):
        there = sel_buf.at[lax.rem(x, 2)]

        @pl.when(sel_keep(hb))
        def _(hb=hb, there=there):
            pltpu.make_async_copy(sel_own.at[hb], there, sel_sem.at[0]).start()

        @pl.when(jnp.logical_not(sel_keep(hb)))
        def _(hb=hb, there=there):
            pltpu.make_async_remote_copy(sel_own.at[hb], there, sel_sem.at[1], sel_sem.at[0],
                                         device_id=head_holder(2 * (yz * 2 + c) + hb, half, zh)).start()

    alls = (k_all, v_all)

    def region(a, p):
        return alls[a].at[pl.ds(p * NB, NB)]

    def hand_on(a, p, slot, target):
        return pltpu.make_async_remote_copy(region(a, p), region(a, p), pass_left.at[a, slot],
                                            pass_arrive.at[a, p], device_id=target)

    for a in range(2):
        whole_wait(alls[a].at[pl.ds(first, NB)], arrive.at[a])

        @pl.when(q == 0)
        def _(a=a):
            hand_on(a, 0, 0, across).start()
            hand_on(a, 0, 1, beside).start()

        @pl.when(q == 1)
        def _(a=a):
            hand_on(a, 1, 0, diagonal).start()
            hand_on(a, 1, 1, beside).start()

        @pl.when(q == 2)
        def _(a=a):
            hand_on(a, 2, 0, across).start()

        if a == 0:
            scatter(2, q_ref, q_buf.at[rows_quarter, :])
            scatter(3, g_ref, g_buf.at[rows_quarter, :])

    for a in range(2):
        @pl.when(q == 1)
        def _(a=a):
            whole_wait(region(a, 0), pass_arrive.at[a, 0])
            hand_on(a, 0, 2, beside).start()

    whole_wait(sel_buf, sel_sem.at[0])
    to_scalars = pltpu.make_async_copy(sel_buf, sel, sel_sem.at[2])
    to_scalars.start()
    for a in range(2):
        @pl.when(q >= 2)
        def _(a=a):
            whole_wait(region(a, 0), pass_arrive.at[a, 0])
            whole_wait(region(a, 1), pass_arrive.at[a, 1])

        @pl.when(q == 3)
        def _(a=a):
            whole_wait(region(a, 2), pass_arrive.at[a, 2])
    to_scalars.wait()
    whole_wait(q_buf, arrive.at[2])

    def rows_of(block):
        return pl.ds(pl.multiple_of(block * BLOCK, BLOCK), BLOCK)

    def chosen(j):
        return [sel[lax.div(j, 2), 0, lax.rem(j, 2) * TOP + t] for t in range(TOP)] + [first + j]

    def live_rows(j):
        at = (first + j) * BLOCK + lax.broadcasted_iota(jnp.int32, (BLOCK, HD), 0)
        return jnp.clip(length_ref[0] - at, 0, 1).astype(jnp.float32)

    def usable(ids, b, t):
        return jnp.minimum(b - ids[t], 1)

    def forward(j, carry):
        b = first + j
        ids = chosen(j)
        queries = q_buf[rows_of(j), :]
        tops = []
        for t in range(SLOTS):
            sc = lax.dot_general(k_all[ids[t]], queries, NT, preferred_element_type=jnp.float32)
            if t == TOP:
                kv = lax.broadcasted_iota(jnp.int32, (BLOCK, BLOCK), 0)
                qp = lax.broadcasted_iota(jnp.int32, (BLOCK, BLOCK), 1)
                sc = jnp.where(kv <= qp, sc, NEG)
            weights[j, t] = sc
            top = jnp.max(sc, axis=0, keepdims=True)
            tops.append(top if t == TOP else top + (1 - usable(ids, b, t)).astype(jnp.float32) * NEG)
        m = jnp.maximum(jnp.maximum(tops[0], tops[1]), jnp.maximum(tops[2], tops[3]))
        total = jnp.zeros((1, BLOCK), jnp.float32)
        for t in range(SLOTS):
            shift = m if t == TOP else m - (1 - usable(ids, b, t)).astype(jnp.float32) * NEG
            p = jnp.exp2((weights[j, t] - shift) * SCALE2)
            total = total + jnp.sum(p, axis=0, keepdims=True)
            weights[j, t] = p
        inv = 1.0 / total
        out_t = jnp.zeros((HD, BLOCK), jnp.float32)
        for t in range(SLOTS):
            w = weights[j, t] * inv
            weights[j, t] = w
            out_t = out_t + lax.dot_general(v_all[ids[t]], w.astype(jnp.bfloat16), TN,
                                            preferred_element_type=jnp.float32)
        o_buf[rows_of(j), :] = (out_t.T * live_rows(j)).astype(jnp.bfloat16)
        return carry
    lax.fori_loop(0, NB, forward, 0)

    column = pl.ds(pl.multiple_of(mine * HD, HD), HD)

    def give(n, src, dst, count, row_at):
        def one(i, carry):
            r = row_at(i)
            piece = src.at[pl.ds(pl.multiple_of(r * ROWS, ROWS), ROWS), :]
            there = dst.at[:, column]
            keep = jnp.logical_and(own, r == start_row)

            @pl.when(keep)
            def _():
                pltpu.make_async_copy(piece, there, arrive_out.at[n]).start()

            @pl.when(jnp.logical_not(keep))
            def _():
                pltpu.make_async_remote_copy(piece, there, left_out.at[n], arrive_out.at[n],
                                             device_id=owner_of(r, half, c)).start()
            return carry
        lax.fori_loop(0, count, one, 0)

    def all_rows(i):
        return lax.rem(start_row + i, PEERS)

    whole_wait(g_buf, arrive.at[3])
    give(0, o_buf, o_out, PEERS, all_rows)

    def grad_of(j):
        return (g_buf[rows_of(j), :].astype(jnp.float32) * live_rows(j)).astype(jnp.bfloat16)

    def value_terms(j, carry):
        g = grad_of(j)
        for t in range(SLOTS):
            terms[j * SLOTS + t] = jnp.dot(weights[j, t].astype(jnp.bfloat16), g, preferred_element_type=jnp.float32)
        return carry

    def combine(a, p):
        def one(i, carry):
            kb = p * NB + i
            acc = jnp.zeros((BLOCK, HD), jnp.float32)
            for j in range(NB):
                ids = chosen(j)
                at = NB * SLOTS
                for t in range(SLOTS):
                    apart = jnp.minimum(jnp.maximum(ids[t] - kb, kb - ids[t]), 1)
                    hit = 1 - apart
                    if t < TOP:
                        hit = hit * usable(ids, first + j, t)
                    at = at + hit * (j * SLOTS + t - NB * SLOTS)
                acc = acc + terms[jnp.clip(at, 0, NB * SLOTS)]
            part[a, rows_of(kb), :] = acc.astype(jnp.bfloat16)
            return carry
        lax.fori_loop(0, NB, one, 0)

    def piece_of(a, p):
        return part.at[a, pl.ds(p * QUARTER, QUARTER), :]

    def send_part(a, p, slot, into, target):
        return pltpu.make_async_remote_copy(piece_of(a, p), got.at[a, into], part_left.at[a, slot],
                                            part_arrive.at[a, into], device_id=target)

    def reduce_out(a):
        for p in range(NB):
            @pl.when(p <= q)
            def _(a=a, p=p):
                combine(a, p)
            if p >= 1:
                @pl.when(q == 3)
                def _(a=a, p=p):
                    into, target = ((2, beside), (1, beside), (0, across))[p - 1]
                    send_part(a, p - 1, p - 1, into, target).start()
                if p <= 2:
                    @pl.when(q == 2)
                    def _(a=a, p=p):
                        into, target = ((1, beside), (0, diagonal))[p - 1]
                        send_part(a, p - 1, p - 1, into, target).start()

    def relay_sum(a):
        whole_wait(got.at[a, 2], part_arrive.at[a, 2])
        relay[a] = (part[a, 0:QUARTER, :].astype(jnp.float32) + got[a, 2].astype(jnp.float32)).astype(jnp.bfloat16)

    def relay_send(a):
        pltpu.make_async_remote_copy(relay.at[a], got.at[a, 0], part_left.at[a, 0],
                                     part_arrive.at[a, 0], device_id=across).start()

    terms[NB * SLOTS] = jnp.zeros((BLOCK, HD), jnp.float32)
    lax.fori_loop(0, NB, value_terms, 0)
    reduce_out(1)

    def backward(j, carry):
        ids = chosen(j)
        g = grad_of(j)
        queries = q_buf[rows_of(j), :]
        delta = jnp.sum((g.astype(jnp.float32) * o_buf[rows_of(j), :].astype(jnp.float32)).T, axis=0, keepdims=True)
        dq_t = jnp.zeros((HD, BLOCK), jnp.float32)
        for t in range(SLOTS):
            dw = lax.dot_general(v_all[ids[t]], g, NT, preferred_element_type=jnp.float32)
            ds = (weights[j, t] * (dw - delta) * SCALE).astype(jnp.bfloat16)
            dq_t = dq_t + lax.dot_general(k_all[ids[t]], ds, TN, preferred_element_type=jnp.float32)
            terms[j * SLOTS + t] = jnp.dot(ds, queries, preferred_element_type=jnp.float32)
        dq_buf[rows_of(j), :] = dq_t.T.astype(jnp.bfloat16)

        @pl.when(jnp.logical_and(q == 1, j == 0))
        def _():
            relay_sum(1)

        @pl.when(jnp.logical_and(q == 1, j == 1))
        def _():
            relay_send(1)

        @pl.when(j >= 1)
        def _():
            give(1, dq_buf, dq_out, per_block, lambda i: (j - 1) * per_block + lax.rem(hh + i, per_block))
        return carry
    lax.fori_loop(0, NB, backward, 0)
    reduce_out(0)
    give(1, dq_buf, dq_out, per_block, lambda i: (NB - 1) * per_block + lax.rem(hh + i, per_block))

    @pl.when(q == 1)
    def _():
        relay_sum(0)

    def finish(a):
        own_rows = pl.ds(pl.multiple_of(q * QUARTER, QUARTER), QUARTER)

        @pl.when(q < 2)
        def _():
            whole_wait(got.at[a, 0], part_arrive.at[a, 0])
            whole_wait(got.at[a, 1], part_arrive.at[a, 1])
            final[a] = (part[a, own_rows, :].astype(jnp.float32) + got[a, 0].astype(jnp.float32)
                        + got[a, 1].astype(jnp.float32)).astype(jnp.bfloat16)

        @pl.when(q == 2)
        def _():
            whole_wait(got.at[a, 0], part_arrive.at[a, 0])
            final[a] = (part[a, own_rows, :].astype(jnp.float32) + got[a, 0].astype(jnp.float32)).astype(jnp.bfloat16)

        @pl.when(q == 3)
        def _():
            final[a] = part[a, own_rows, :]

    finish(1)

    @pl.when(q == 1)
    def _():
        relay_send(0)
    give(3, final.at[1], dv_out, PEERS, all_rows)
    finish(0)
    give(2, final.at[0], dk_out, PEERS, all_rows)

    for n, out in enumerate((o_out, dq_out, dk_out, dv_out)):
        whole_wait(out, arrive_out.at[n])
    for a in range(2):
        for where, sems in ((0, (pass_left.at[a, 0], pass_left.at[a, 1])),
                            (1, (pass_left.at[a, 0], pass_left.at[a, 1], pass_left.at[a, 2], part_left.at[a, 0])),
                            (2, (pass_left.at[a, 0], part_left.at[a, 0], part_left.at[a, 1])),
                            (3, (part_left.at[a, 0], part_left.at[a, 1], part_left.at[a, 2]))):
            @pl.when(q == where)
            def _(sems=sems):
                for sem in sems:
                    whole_wait(q_buf, sem)
    most = q_buf.at[pl.ds(0, QUARTER - ROWS), :]
    last = q_buf.at[pl.ds(0, ROWS), :]
    for sems in (left, left_out):
        for n in range(4):
            whole_wait(most, sems.at[n])

            @pl.when(jnp.logical_not(own))
            def _(n=n, sems=sems):
                whole_wait(last, sems.at[n])
    for hb in range(2):
        @pl.when(jnp.logical_not(sel_keep(hb)))
        def _(hb=hb):
            whole_wait(sel_own.at[hb], sel_sem.at[1])


ANY = pl.BlockSpec(memory_space=pl.ANY)
SMEM = pl.BlockSpec(memory_space=pltpu.SMEM)


def body(queries, keys, values, out_grad, selected, length):
    low = jnp.bfloat16
    dma = pltpu.SemaphoreType.DMA
    vmem = pltpu.VMEM
    owned = jax.ShapeDtypeStruct((ROWS, HEADS * HD), low)
    return pl.pallas_call(
        fused_kernel,
        out_shape=(owned,) * 4,
        in_specs=[ANY] * 4 + [SMEM] * 2,
        out_specs=(ANY,) * 4,
        scratch_shapes=[vmem((NBLK, BLOCK, HD), low), vmem((NBLK, BLOCK, HD), low)] + [vmem((QUARTER, HD), low)] * 4
        + [vmem((2, 8, 128), jnp.int32), vmem((2, 8, 128), jnp.int32), pltpu.SMEM((2, 8, 128), jnp.int32),
           vmem((NB, SLOTS, BLOCK, BLOCK), jnp.float32), vmem((NB * SLOTS + 1, BLOCK, HD), jnp.float32),
           vmem((2, TOKENS, HD), low), vmem((2, 3, QUARTER, HD), low), vmem((2, QUARTER, HD), low),
           vmem((2, QUARTER, HD), low),
           dma((4,)), dma((4,)), dma((2, 3)), dma((2, 3)), dma((3,)), dma((4,)), dma((4,)), dma((2, 3)), dma((2, 3))],
        compiler_params=pltpu.CompilerParams(collective_id=0, has_side_effects=True,
                                             vmem_limit_bytes=60 * 1024 * 1024),
        name="fused",
    )(keys, values, queries, out_grad, selected, length)


def solution(mesh):
    rows = P(("seq", "head"), None)
    return jax.shard_map(
        body,
        mesh=mesh,
        in_specs=(rows, rows, rows, rows, P("head", "seq", None), P()),
        out_specs=(rows, rows, rows, rows),
        check_vma=False,
    )
```

time: 149 us -> 118 us (0.79)
  Pallas kernels: 137 us -> 111 us
  local copies, waits for them, and re-layouts: 9.8 us -> 5.18 us
    pallas_call x3 -> x1, Pallas kernels: 137 us -> 111 us  [body(): pl.pallas_call(fused_kernel, out_shape=(owned,) * 4, in_specs=[ANY] * 4 +...]
    unnamed x12 -> x10, local copies, waits for them, and re-layouts: 8.44 us -> 5.18 us
where the time goes in v2:
time: 118 us; the launch traced here: 117 us
  Pallas kernels  111 us (94%)
  local copies, waits for them, and re-layouts  5.18 us (4%)
  between operations  1.3 us (1%)
    pallas_call x1, Pallas kernels, body(): pl.pallas_call(fused_kernel, out_shape=(owned,) * 4, in_specs=[ANY] * 4 +...  111 us
    unnamed x10, local copies, waits for them, and re-layouts  5.18 us

profile of v2, /device:TPU:1, one launch (start us, length us, event | category | flops | bytes accessed | tf_op | source)
XLA Modules:
  0.0 117.3 jit_solution(16576626363078529872)
XLA Ops:
  1.3 110.9 %fused.1 = (bf16[32,8192]{1,0:T(8,128)(2,1)}, bf16[32,8192]{1,0:T(8,128)(2,1)}, bf16[32,8192]{1,0:T(8,128)(2,1)}, bf16[32,8192]{1,0:T(8,128)(2,1)}) custom-call(bf16[32,8192]{1,0:T(8,128)(2,1)} %k_ref.1, bf16[32,8192]{1,0:T(8,128)(2,1)} %v_ref.1, bf16[32,8192]{1,0:T(8,128)(2,1)} %q_ref.1, bf16[32,8192]{1,0:T(8,128)(2,1)} %g_ref.1, s32[2,2,3]{2,1,0:T(2,128)} %chosen_ref.1, ...), custom_call_target="tpu_custom_call" | custom-call | tf_op jit(solution)/shard_map/fused/pallas_call | solution.py:420
  112.2 0.0 copy-start.2
  112.2 1.9 %copy.15 = bf16[32,8192]{1,0:T(8,128)(2,1)} copy(bf16[32,8192]{1,0:T(8,128)(2,1)} %get-tuple-element.8) | data formatting | bytes 1048576
  114.1 0.0 copy-done.2
  114.1 0.0 copy-start.1
  114.1 0.8 copy.16
  114.9 0.4 copy-done.1
  115.3 0.0 copy-start
  115.3 0.8 copy.17
  116.1 0.4 copy-done
  116.6 0.8 copy.18
Async XLA Ops:
  112.2 1.9 %copy-start.2 = (bf16[32,8192]{1,0:T(8,128)(2,1)S(1)}, bf16[32,8192]{1,0:T(8,128)(2,1)}, u32[]{:S(2)}) copy-start(bf16[32,8192]{1,0:T(8,128)(2,1)} %get-tuple-element.9) | copy-start | bytes 1572868
  114.1 1.2 %copy-start.1 = (bf16[32,8192]{1,0:T(8,128)(2,1)S(1)}, bf16[32,8192]{1,0:T(8,128)(2,1)}, u32[]{:S(2)}) copy-start(bf16[32,8192]{1,0:T(8,128)(2,1)} %get-tuple-element.10) | copy-start | bytes 1572868
  115.3 1.2 %copy-start = (bf16[32,8192]{1,0:T(8,128)(2,1)S(1)}, bf16[32,8192]{1,0:T(8,128)(2,1)}, u32[]{:S(2)}) copy-start(bf16[32,8192]{1,0:T(8,128)(2,1)} %get-tuple-element.11) | copy-start | bytes 1572868
